TPU v7x, 32 devices: a whole 2x2x4 slice. The times are simulated.
32 devices in a mesh: row: 2 (over y), col: 16 (over z, x, core).
Axes of the slice: x: 2, y: 2, z: 4, core: 2. Of those that a mesh axis runs over, the one named last changes fastest.
Arguments:
- start_block: float32 [32, 8192], P(None, 'col'), may hold values from -6 to 6
- energies: float32 [8192], P('col'), may hold values from 1 to 10
- hamiltonian: float32 [16, 16, 512, 512], P('row', 'col'), may hold values from -0.125 to 0.125
Outputs:
- recurrence: float32 [2, 2, 32, 32], replicated
- next_block: float32 [32, 8192], P(None, 'col')
All inputs are finite; a program needn't handle non-finite values.
Results may differ from a plain program's by a relative error of at most 0.0003.
Values sent between devices are 32-bit elements; how exact they have to be, the bound alone decides.
A program may use at most 64 MiB of HBM per device.

v0:
```python
import jax
import jax.numpy as jnp
from jax import lax
from jax.sharding import PartitionSpec as P

ITERS = 2


FULL_PRECISION = lax.Precision.HIGHEST


def mean_inner(left, right):
    length = lax.axis_size("col") * left.shape[1]
    return lax.psum(jnp.dot(left, right.T, precision=FULL_PRECISION), "col") / length


def normalize(block):
    factor = jnp.linalg.cholesky(mean_inner(block, block))
    return (lax.linalg.triangular_solve(factor, block, left_side=True, lower=True), factor)


def on_device(start_block, energies, hamiltonian):
    row_index = lax.axis_index("row")
    col_index = lax.axis_index("col")
    row_count = lax.axis_size("row")
    col_count = lax.axis_size("col")
    slot_count = hamiltonian.shape[0]
    width = hamiltonian.shape[2]
    vec_count = start_block.shape[0]
    blocks = hamiltonian[:, 0]
    block_rows = row_index + row_count * jnp.arange(slot_count, dtype=jnp.int32)
    weight = jnp.where(
        block_rows < col_index,
        jnp.float32(1.0),
        jnp.where(block_rows == col_index, jnp.float32(0.5), jnp.float32(0.0)),
    )
    selector = (block_rows[:, None] == jnp.arange(col_count, dtype=jnp.int32)[None, :]).astype(
        jnp.float32
    )
    current, factor = normalize(start_block)
    previous = jnp.zeros_like(current)
    last_factor = jnp.zeros((vec_count, vec_count), jnp.float32)
    history = []
    for iteration in range(ITERS):
        whole = lax.all_gather(current, "col", axis=1, tiled=True).reshape(
            vec_count, col_count, width
        )
        chosen = jnp.take(whole, block_rows, axis=1) * weight[None, :, None]
        downward = jnp.einsum("psk,skl->pl", chosen, blocks, precision=FULL_PRECISION)
        across = (
            jnp.einsum("pl,skl->spk", current, blocks, precision=FULL_PRECISION)
            * weight[:, None, None]
        )
        spread = jnp.einsum("sj,spk->pjk", selector, across, precision=FULL_PRECISION).reshape(
            vec_count, col_count * width
        )
        mine = lax.psum_scatter(spread, "col", scatter_dimension=1, tiled=True)
        column_total = lax.psum(downward + mine, "row")
        residual_block = (
            column_total
            + energies[None, :] * current
            - jnp.dot(last_factor.T, previous, precision=FULL_PRECISION)
        )
        diagonal_block = mean_inner(residual_block, current)
        residual_block = residual_block - jnp.dot(diagonal_block, current, precision=FULL_PRECISION)
        following, new_factor = normalize(residual_block)
        history.append(jnp.stack([diagonal_block, new_factor]))
        previous, current, last_factor = (current, following, new_factor)
    return (jnp.stack(history), current)


def solution(mesh):
    placed = (P(None, "col"), P("col"), P("row", "col", None, None))
    return jax.shard_map(
        on_device, mesh=mesh, in_specs=placed, out_specs=(P(), P(None, "col")), check_vma=False
    )
```

profile of v0, /device:TPU:0, one launch (start us, length us, event | category | flops | bytes accessed | tf_op | source)
XLA Modules:
  0.0 588.7 jit_solution(12538500507345331128)
XLA Ops:
  8.2 63.0 %psum.49 = f32[32,32]{1,0:T(8,128)S(1)} all-reduce(f32[32,32]{1,0:T(8,128)S(1)} %fusion.79), channel_id=1, replica_groups=mesh['row'=2,'col'=16] {'col'}, use_global_device_ids=true, to_apply=%region_0.1 | all-reduce | flops 1024 | bytes 8192 | tf_op jit(solution)/shard_map/psum | solution.py:14
  71.3 2.9 cholesky.59
  75.6 2.5 custom-call.7
  79.0 10.0 %fusion.11 = f32[8,32,512]{2,1,0:T(8,128)S(1)} fusion(f32[8,1,512,512]{3,2,1,0:T(8,128)} %param.10, f32[8]{0:T(128)S(1)} %compare_select_fusion.2, f32[32,512]{1,0:T(8,128)} %fusion.54), kind=kOutput, calls=%fused_computation.11 | convolution fusion | flops 805437440 | bytes 8978464 | tf_op jit(solution)/shard_map/pl,skl->spk/dot_general | solution.py:51
  89.9 1.6 copy.25
  91.7 22.6 %all-gather.3.cloned.1.call-done = f32[32,8192]{1,0:T(8,128)} async-done(((f32[32,512]{1,0:T(8,128)}), f32[32,8192]{1,0:T(8,128)}) %all-gather.3.cloned.1.call-update) | async-done | bytes 1048592 | tf_op jit(solution)/shard_map/all_gather | solution.py:45
  116.2 58.3 %reduce-scatter.3.cloned.1.call-done = f32[32,512]{1,0:T(8,128)} async-done(((f32[32,8192]{1,0:T(8,128)}), f32[32,512]{1,0:T(8,128)}) %reduce-scatter.3.cloned.1.call-update) | async-done | bytes 65552 | tf_op jit(solution)/shard_map/reduce_scatter | solution.py:57
  174.5 7.8 %fusion.29 = f32[32,512]{1,0:T(8,128)} fusion(f32[32,512]{1,0:T(8,128)} %reduce-scatter.3.cloned.1.call-done, f32[8,1,512,512]{3,2,1,0:T(8,128)} %param.10, f32[8,32,512]{2,1,0:T(8,128)S(1)} %gather_fusion, f32[8]{0:T(128)S(1)} %compare_select_fusion.2, pred[8]{0:T(512)(128)(4,1)S(1)} %compare_and_fusion), kind=kOutput, calls=%fused_computation.21 | convolution fusion | flops 805584896 | bytes 9044008 | tf_op jit(solution)/shard_map/psk,skl->pl/dot_general | solution.py:49
  182.4 20.1 %all-reduce.3.cloned.1.call-done = f32[32,512]{1,0:T(8,128)} async-done(((f32[32,512]{1,0:T(8,128)}), f32[32,512]{1,0:T(8,128)}) %all-reduce.3.cloned.1.call-update) | async-done | bytes 65552 | tf_op jit(solution)/shard_map/psum | solution.py:58
  203.7 60.7 %psum.51 = f32[32,32]{1,0:T(8,128)S(1)} all-reduce(f32[32,32]{1,0:T(8,128)S(1)} %fusion.80), channel_id=1, replica_groups=mesh['row'=2,'col'=16] {'col'}, use_global_device_ids=true, to_apply=%region_5.9 | all-reduce | flops 1024 | bytes 8192 | tf_op jit(solution)/shard_map/psum | solution.py:14
  264.9 57.6 %psum.52 = f32[32,32]{1,0:T(8,128)S(1)} all-reduce(f32[32,32]{1,0:T(8,128)S(1)} %fusion.81), channel_id=1, replica_groups=mesh['row'=2,'col'=16] {'col'}, use_global_device_ids=true, to_apply=%region_6.10 | all-reduce | flops 1024 | bytes 8192 | tf_op jit(solution)/shard_map/psum | solution.py:14
  322.6 2.9 cholesky.70
  326.9 2.5 custom-call.8
  330.5 10.0 %fusion.17 = f32[8,32,512]{2,1,0:T(8,128)S(1)} fusion(f32[8,1,512,512]{3,2,1,0:T(8,128)} %param.10, f32[8]{0:T(128)S(1)} %compare_select_fusion.2, f32[32,512]{1,0:T(8,128)} %fusion.51), kind=kOutput, calls=%fused_computation.13 | convolution fusion | flops 805437440 | bytes 8978464 | tf_op jit(solution)/shard_map/pl,skl->spk/dot_general | solution.py:51
  341.4 1.6 copy.26
  343.1 21.5 %all-gather.5.cloned.1.call-done = f32[32,8192]{1,0:T(8,128)} async-done(((f32[32,512]{1,0:T(8,128)}), f32[32,8192]{1,0:T(8,128)}) %all-gather.5.cloned.1.call-update) | async-done | bytes 1048592 | tf_op jit(solution)/shard_map/all_gather | solution.py:45
  366.5 58.2 %reduce-scatter.5.cloned.1.call-done = f32[32,512]{1,0:T(8,128)} async-done(((f32[32,8192]{1,0:T(8,128)}), f32[32,512]{1,0:T(8,128)}) %reduce-scatter.5.cloned.1.call-update) | async-done | bytes 65552 | tf_op jit(solution)/shard_map/reduce_scatter | solution.py:57
  424.7 7.8 %fusion.26 = f32[32,512]{1,0:T(8,128)} fusion(f32[32,512]{1,0:T(8,128)} %reduce-scatter.5.cloned.1.call-done, f32[8,1,512,512]{3,2,1,0:T(8,128)} %param.10, f32[8,32,512]{2,1,0:T(8,128)S(1)} %gather_fusion.1, f32[8]{0:T(128)S(1)} %compare_select_fusion.2, pred[8]{0:T(512)(128)(4,1)S(1)} %compare_and_fusion), kind=kOutput, calls=%fused_computation.20 | convolution fusion | flops 805584896 | bytes 9044008 | tf_op jit(solution)/shard_map/psk,skl->pl/dot_general | solution.py:49
  432.6 20.2 %all-reduce.5.cloned.1.call-done = f32[32,512]{1,0:T(8,128)} async-done(((f32[32,512]{1,0:T(8,128)}), f32[32,512]{1,0:T(8,128)}) %all-reduce.5.cloned.1.call-update) | async-done | bytes 65552 | tf_op jit(solution)/shard_map/psum | solution.py:58
  452.7 1.7 convolution_subtract_fusion.1
  454.7 60.7 %psum.54 = f32[32,32]{1,0:T(8,128)S(1)} all-reduce(f32[32,32]{1,0:T(8,128)S(1)} %fusion.82), channel_id=1, replica_groups=mesh['row'=2,'col'=16] {'col'}, use_global_device_ids=true, to_apply=%region_9.13 | all-reduce | flops 1024 | bytes 8192 | tf_op jit(solution)/shard_map/psum | solution.py:14
  515.8 57.6 %psum.55 = f32[32,32]{1,0:T(8,128)S(1)} all-reduce(f32[32,32]{1,0:T(8,128)S(1)} %fusion.83), channel_id=1, replica_groups=mesh['row'=2,'col'=16] {'col'}, use_global_device_ids=true, to_apply=%region_10.14 | all-reduce | flops 1024 | bytes 8192 | tf_op jit(solution)/shard_map/psum | solution.py:14
  573.6 2.9 cholesky.81
  577.9 2.4 custom-call.9
  (68 shorter events, 17.0 us)
Async XLA Ops:
  7.2 0.8 copy-start
  7.2 107.1 %all-gather.3.cloned.1.call-start = ((), (), s32[]{:S(2)}) async-start(), calls=%async_computation.2 | async-start | bytes 1114112 | tf_op jit(solution)/shard_map/all_gather | solution.py:45
  79.0 95.5 %reduce-scatter.3.cloned.1.call-start = ((), (), s32[]{:S(2)}) async-start(), calls=%async_computation.3 | async-start | bytes 1114112 | tf_op jit(solution)/shard_map/reduce_scatter | solution.py:57
  89.0 113.5 %copy-start.1 = (f32[32,512]{1,0:T(8,128)S(1)}, f32[32,512]{1,0:T(8,128)}, u32[]{:S(2)}) copy-start(f32[32,512]{1,0:T(8,128)} %fusion.54) | copy-start | bytes 196612
  89.0 113.5 %copy-start.3 = (f32[512]{0:T(512)S(1)}, f32[512]{0:T(512)}, u32[]{:S(2)}) copy-start(f32[512]{0:T(512)} %param.9) | copy-start | bytes 6148
  91.6 110.9 %all-reduce.3.cloned.1.call-start = ((), (), s32[]{:S(2)}) async-start(), calls=%async_computation.4 | async-start | bytes 131072 | tf_op jit(solution)/shard_map/psum | solution.py:58
  182.3 182.3 %all-gather.5.cloned.1.call-start = ((), (), s32[]{:S(2)}) async-start(), calls=%async_computation.5 | async-start | bytes 1114112 | tf_op jit(solution)/shard_map/all_gather | solution.py:45
  330.3 94.4 %reduce-scatter.5.cloned.1.call-start = ((), (), s32[]{:S(2)}) async-start(), calls=%async_computation.6 | async-start | bytes 1114112 | tf_op jit(solution)/shard_map/reduce_scatter | solution.py:57
  340.5 112.2 %copy-start.2 = (f32[32,512]{1,0:T(8,128)S(1)}, f32[32,512]{1,0:T(8,128)}, u32[]{:S(2)}) copy-start(f32[32,512]{1,0:T(8,128)} %fusion.51) | copy-start | bytes 196612
  343.1 109.7 %all-reduce.5.cloned.1.call-start = ((), (), s32[]{:S(2)}) async-start(), calls=%async_computation.7 | async-start | bytes 131072 | tf_op jit(solution)/shard_map/psum | solution.py:58
Sparse Core Ops, SparseCore 0:
  79.1 35.1 all-gather.2
  117.9 56.5 reduce-scatter.2
  182.5 20.0 all-reduce.2
  330.4 34.1 all-gather.4
  368.1 56.5 reduce-scatter.4
  432.7 20.0 all-reduce.4
where the time goes:
time: 589 us
  blocking collectives  300 us (51%)
  waiting for transfers between devices  201 us (34%)
  matrix products  44 us (7%)
  other arithmetic  20.9 us (4%)
  between operations  14.4 us (2%)
  local copies, waits for them, and re-layouts  8.33 us (1%)
    psum x5, blocking collectives, mean_inner(): lax.psum(jnp.dot(left, right.T, precision=FULL_PRECISION), 'col') / length  300 us
    reduce_scatter x2, waiting for transfers between devices, on_device(): mine = lax.psum_scatter(spread, 'col', scatter_dimension=1, tiled=True)  117 us
    all_gather x2, waiting for transfers between devices, on_device(): lax.all_gather(current, 'col', axis=1, tiled=True)  44.1 us
    psum x2, waiting for transfers between devices, on_device(): column_total = lax.psum(downward + mine, 'row')  40.3 us
    dot_general x2, matrix products, on_device(): jnp.einsum('pl,skl->spk', current, blocks, precision=FULL_PRECISION)  19.9 us
    dot_general x2, matrix products, on_device(): jnp.einsum('psk,skl->pl', chosen, blocks, precision=FULL_PRECISION)  15.6 us
  transfers between devices with their start and end apart: 6, of which 6 were waited for; matrix products, arithmetic and copies ran while one was open for 5% of the time, Pallas kernels for 0%

commit v1 on v0

v1 whole, which is shorter than its diff:
```python
import functools

import jax
import jax.numpy as jnp
from jax import lax
from jax.experimental import pallas as pl
from jax.experimental.pallas import tpu as pltpu
from jax.sharding import PartitionSpec as P

ITERS = 2
LANES = 128
MESH = pl.DeviceIdType.MESH
F32 = jnp.float32
BF16 = jnp.bfloat16


def full_dot(left, right, contract):
    return lax.dot_general(
        left, right, (contract, ((), ())), precision=lax.Precision.HIGHEST, preferred_element_type=F32
    )


def split(value):
    high = value.astype(BF16)
    return high, (value - high.astype(F32)).astype(BF16)


def stacked_split(value):
    return jnp.concatenate(split(value), axis=0)


def three_products(stacked, high, low, contract):
    vecs = stacked.shape[0] // 2
    dims = (contract, ((), ()))
    both = lax.dot_general(stacked, high, dims, preferred_element_type=F32)
    extra = lax.dot_general(stacked[:vecs], low, dims, preferred_element_type=F32)
    return both[:vecs] + (both[vecs:] + extra)


def placed_rows(value, slot):
    vecs, width = value.shape
    parts = [jnp.zeros((vecs, width), F32)] * (LANES // vecs)
    parts[slot] = value
    return jnp.concatenate(parts, axis=0)


def factor_and_inverse(gram, row, lane, vecs):
    work = jnp.where(lane < vecs, gram, (lane - vecs == row).astype(F32))
    for step in range(vecs):
        scale = lax.rsqrt(work[step : step + 1, step : step + 1])
        pivot_row = work[step : step + 1, :] * scale
        column = work[:, step : step + 1] * scale
        work = jnp.where(
            row > step, work - column * pivot_row, jnp.where(row == step, pivot_row, work)
        )
    return work


def kernel(
    rows, cols, group,
    x_ref, e_ref, h_ref, rec_ref, next_ref,
    h_buf, h_high, h_low, lhs_buf, w_buf, gathered, across_out, across_in, acc, own, row_parts, gram_one, gram_two,
    h_sem, gather_send, gather_recv, across_send, across_recv, row_send, row_recv, one_send, one_recv, two_send, two_recv,
):
    r, c = lax.axis_index("row"), lax.axis_index("col")
    slots = h_ref.shape[0]
    vecs, width = x_ref.shape
    length = F32(cols * width)
    member, team = c % group, c // group
    teams = cols // group
    is_owner = (c % rows) == r
    row = lax.broadcasted_iota(jnp.int32, (vecs, LANES), 0)
    lane = lax.broadcasted_iota(jnp.int32, (vecs, LANES), 1)

    def remote(src, dst, send, recv, where):
        return pltpu.make_async_remote_copy(
            src_ref=src, dst_ref=dst, send_sem=send, recv_sem=recv, device_id=where, device_id_type=MESH
        )

    def loop(count, start=0):
        def wrap(body):
            lax.fori_loop(start, count, lambda i, _: (body(i), 0)[1], 0)
        return wrap

    def h_copy(i):
        return pltpu.make_async_copy(h_ref.at[i, 0], h_buf.at[i], h_sem.at[i])

    barrier = pltpu.get_barrier_semaphore()

    @loop(cols)
    def _(other):
        @pl.when(other != c)
        def _():
            pl.semaphore_signal(barrier, inc=1, device_id=(r, other), device_id_type=MESH)

    @loop(rows)
    def _(other):
        @pl.when(other != r)
        def _():
            pl.semaphore_signal(barrier, inc=1, device_id=(other, c), device_id_type=MESH)

    @loop(slots)
    def _(i):
        @pl.when(i * rows + r <= c)
        def _():
            h_copy(i).start()

    def one_copy(k, other):
        return remote(
            gram_one.at[k, member], gram_one.at[k, member], one_send.at[k, other], one_recv.at[k, member],
            (r, team * group + other),
        )

    def one_wait(k, other):
        return remote(
            gram_one.at[k, other], gram_one.at[k, other], one_send.at[k, other], one_recv.at[k, other],
            (r, team * group + other),
        )

    def two_copy(k, other):
        return remote(
            gram_two.at[k, team], gram_two.at[k, team], two_send.at[k, other], two_recv.at[k, team],
            (r, other * group + member),
        )

    def two_wait(k, other):
        return remote(
            gram_two.at[k, other], gram_two.at[k, other], two_send.at[k, other], two_recv.at[k, other],
            (r, other * group + member),
        )

    def gram_start(k, value):
        gram_one[k, member] = value

        @loop(group)
        def _(other):
            @pl.when(other != member)
            def _():
                one_copy(k, other).start()

    def gram_middle(k):
        @loop(group)
        def _(other):
            @pl.when(other != member)
            def _():
                one_wait(k, other).wait_recv()

        total = gram_one[k, 0]
        for other in range(1, group):
            total = total + gram_one[k, other]
        gram_two[k, team] = total

        @loop(teams)
        def _(other):
            @pl.when(other != team)
            def _():
                two_copy(k, other).start()

    def gram_end(k):
        @loop(teams)
        def _(other):
            @pl.when(other != team)
            def _():
                two_wait(k, other).wait_recv()

        total = gram_two[k, 0]
        for other in range(1, teams):
            total = total + gram_two[k, other]
        return total

    def gather_copy(app, src, other):
        slot = c // rows
        return remote(
            src, gathered.at[app, slot], gather_send.at[app, other], gather_recv.at[app, slot], (r, other)
        )

    def gather_wait(app, i):
        return remote(
            gathered.at[app, i], gathered.at[app, i], gather_send.at[app, 0], gather_recv.at[app, i], (r, i * rows + r)
        )

    def across_copy(app, i):
        return remote(
            across_out.at[app, i], across_in.at[app, c], across_send.at[app, i], across_recv.at[app, c],
            (r, i * rows + r),
        )

    def across_wait(app, other):
        return remote(
            across_in.at[app, other], across_in.at[app, other], across_send.at[app, 0], across_recv.at[app, other],
            (r, other),
        )

    def row_copy(app, other):
        return remote(
            row_parts.at[app, r], row_parts.at[app, r], row_send.at[app, other], row_recv.at[app, r], (other, c)
        )

    def row_wait(app, other):
        return remote(
            row_parts.at[app, other], row_parts.at[app, other], row_send.at[app, other], row_recv.at[app, other],
            (other, c),
        )

    def send_block(app, src):
        @pl.when(is_owner)
        def _():
            gathered[app, c // rows] = 0.5 * src[...]

            @loop(cols, c + 1)
            def _(other):
                gather_copy(app, src, other).start()

    def send_across(app, src):
        lhs_buf[...] = stacked_split(src[...])

        @loop(slots)
        def _(i):
            block_row = i * rows + r

            @pl.when(block_row <= c)
            def _():
                if app == 0:
                    h_copy(i).wait()
                    high, low = split(h_buf[i])
                    h_high[i] = high
                    h_low[i] = low
                else:
                    high, low = h_high[i], h_low[i]
                piece = three_products(lhs_buf[...], high, low, ((1,), (1,)))

                @pl.when(block_row < c)
                def _():
                    across_out[app, i] = piece
                    across_copy(app, i).start()

                @pl.when(block_row == c)
                def _():
                    own[...] = 0.5 * piece

    def downward(app):
        acc[...] = jnp.zeros_like(acc)

        @loop(slots)
        def _(i):
            block_row = i * rows + r

            @pl.when(block_row < c)
            def _():
                gather_wait(app, i).wait_recv()

            @pl.when(block_row <= c)
            def _():
                acc[...] += three_products(
                    stacked_split(gathered[app, i]), h_high[i], h_low[i], ((1,), (0,))
                )

    def collect(app):
        @pl.when(is_owner)
        def _():
            acc[...] += own[...]

            @loop(cols, c + 1)
            def _(other):
                across_wait(app, other).wait_recv()
                acc[...] += across_in[app, other]

        row_parts[app, r] = acc[...]

        @loop(rows)
        def _(other):
            @pl.when(other != r)
            def _():
                row_copy(app, other).start()

    def row_total(app):
        @loop(rows)
        def _(other):
            @pl.when(other != r)
            def _():
                row_wait(app, other).wait_recv()

        total = row_parts[app, 0]
        for other in range(1, rows):
            total = total + row_parts[app, other]
        return total

    in_second = (lane >= vecs) & (lane < 2 * vecs)

    def first_part(matrix):
        return jnp.where(lane < vecs, matrix, 0.0)

    def second_part(matrix):
        return jnp.where(in_second, matrix, 0.0)

    def apply_first(matrix, block):
        return full_dot(first_part(matrix), placed_rows(block, 0), ((1,), (0,)))

    def apply_second(matrix, block):
        return full_dot(second_part(matrix), placed_rows(block, 1), ((1,), (0,)))

    def gram_pair(left, other):
        zero = jnp.zeros((LANES - 2 * vecs, width), F32)
        right = jnp.concatenate([left, other, zero], axis=0)
        return full_dot(left, right, ((1,), (1,))) / length

    def residual_gram(pair):
        part = second_part(pair)
        return pair - full_dot(part, placed_rows(part, 0), ((1,), (1,)))

    def record(k, pair, work, sigma):
        diagonal = pltpu.roll(pair, LANES - vecs, axis=1) + jnp.where(lane == row, sigma, 0.0)
        rec_ref[k, 0] = diagonal[:, :vecs]
        upper = jnp.where(lane >= row, first_part(work), 0.0)
        rec_ref[k, 1] = placed_rows(upper, 0).T[:vecs, :vecs]

    energy = e_ref[...]
    start = x_ref[...]
    zero_block = jnp.zeros_like(start)
    local = gram_pair(start, zero_block) + jnp.where(lane == 2 * vecs, jnp.sum(energy) / length, 0.0)

    pl.semaphore_wait(barrier, cols - 1 + rows - 1)
    send_block(0, x_ref)
    gram_start(0, local)
    send_across(0, x_ref)
    gram_middle(0)
    downward(0)
    pair = gram_end(0)
    sigma = pair[0:1, 2 * vecs : 2 * vecs + 1]
    work = factor_and_inverse(pair, row, lane, vecs)
    current = apply_second(work, start)
    collect(0)
    image = apply_second(work, row_total(0) + energy * start)
    w_buf[...] = image - sigma * current

    send_block(1, w_buf)
    shifted = w_buf[...]
    gram_start(1, gram_pair(shifted, current))
    send_across(1, w_buf)
    gram_middle(1)
    downward(1)
    pair = gram_end(1)
    work = factor_and_inverse(residual_gram(pair), row, lane, vecs)
    record(0, pair, work, sigma)
    following = apply_second(work, shifted - apply_second(pair, current))
    collect(1)
    w_image = row_total(1) + energy * shifted
    following_image = apply_second(work, w_image - apply_second(pair, image))
    last = following_image - apply_first(work, current) - sigma * following
    gram_start(2, gram_pair(last, following))
    gram_middle(2)
    pair = gram_end(2)
    work = factor_and_inverse(residual_gram(pair), row, lane, vecs)
    record(1, pair, work, sigma)
    next_ref[...] = apply_second(work, last - apply_second(pair, following))

    for app in range(ITERS):
        source = x_ref if app == 0 else w_buf

        @pl.when(is_owner)
        def _():
            @loop(cols, c + 1)
            def _(other):
                gather_copy(app, source, other).wait_send()

        @loop(slots)
        def _(i):
            @pl.when(i * rows + r < c)
            def _():
                across_copy(app, i).wait_send()

        @loop(rows)
        def _(other):
            @pl.when(other != r)
            def _():
                row_copy(app, other).wait_send()

    for k in range(ITERS + 1):
        @loop(group)
        def _(other):
            @pl.when(other != member)
            def _():
                one_copy(k, other).wait_send()

        @loop(teams)
        def _(other):
            @pl.when(other != team)
            def _():
                two_copy(k, other).wait_send()


def solution(mesh):
    rows, cols = mesh.shape["row"], mesh.shape["col"]
    group = 1
    while group * group * 4 <= cols and cols % (2 * group) == 0:
        group *= 2

    def on_device(start_block, energies, hamiltonian):
        vecs, width = start_block.shape
        slots = hamiltonian.shape[0]
        vmem = pl.BlockSpec(memory_space=pltpu.VMEM)
        dma = pltpu.SemaphoreType.DMA
        teams = cols // group
        block = (vecs, width)
        grams = ITERS + 1
        return pl.pallas_call(
            functools.partial(kernel, rows, cols, group),
            out_shape=(
                jax.ShapeDtypeStruct((ITERS, 2, vecs, vecs), F32),
                jax.ShapeDtypeStruct(block, F32),
            ),
            in_specs=[vmem, vmem, pl.BlockSpec(memory_space=pl.ANY)],
            out_specs=(vmem, vmem),
            scratch_shapes=[
                pltpu.VMEM((slots, width, width), F32),
                pltpu.VMEM((slots, width, width), BF16),
                pltpu.VMEM((slots, width, width), BF16),
                pltpu.VMEM((2 * vecs, width), BF16),
                pltpu.VMEM(block, F32),
                pltpu.VMEM((ITERS, slots) + block, F32),
                pltpu.VMEM((ITERS, slots) + block, F32),
                pltpu.VMEM((ITERS, cols) + block, F32),
                pltpu.VMEM(block, F32),
                pltpu.VMEM(block, F32),
                pltpu.VMEM((ITERS, rows) + block, F32),
                pltpu.VMEM((grams, group, vecs, LANES), F32),
                pltpu.VMEM((grams, teams, vecs, LANES), F32),
                dma((slots,)),
                dma((ITERS, cols)),
                dma((ITERS, slots)),
                dma((ITERS, slots)),
                dma((ITERS, cols)),
                dma((ITERS, rows)),
                dma((ITERS, rows)),
                dma((grams, group)),
                dma((grams, group)),
                dma((grams, teams)),
                dma((grams, teams)),
            ],
            compiler_params=pltpu.CompilerParams(
                collective_id=0, has_side_effects=True, vmem_limit_bytes=56 << 20
            ),
        )(start_block, energies.reshape(1, width), hamiltonian)

    placed = (P(None, "col"), P("col"), P("row", "col", None, None))
    return jax.shard_map(
        on_device, mesh=mesh, in_specs=placed, out_specs=(P(), P(None, "col")), check_vma=False
    )
```

time: 589 us -> 66 us (0.11)
  blocking collectives: 300 us -> 0 us
  waiting for transfers between devices: 201 us -> 0 us
  Pallas kernels: 0 us -> 61.8 us
  matrix products: 44 us -> 0 us
  other arithmetic: 20.9 us -> 0 us
  between operations: 14.4 us -> 0.64 us
    psum x5 -> x0, blocking collectives: 300 us -> none  [mean_inner(): lax.psum(jnp.dot(left, right.T, precision=FULL_PRECISION), 'col') / length]
    reduce_scatter x2 -> x0, waiting for transfers between devices: 117 us -> none  [on_device(): mine = lax.psum_scatter(spread, 'col', scatter_dimension=1, tiled=True)]
    pallas_call x0 -> x1, Pallas kernels: none -> 61.8 us  [on_device(): pl.pallas_call(functools.partial(kernel, rows, cols, group), out_shape=(j...]
    all_gather x2 -> x0, waiting for transfers between devices: 44.1 us -> none  [on_device(): lax.all_gather(current, 'col', axis=1, tiled=True)]
    dot_general x15 -> x0, matrix products: 41.3 us -> none  [the longest x2 19.9 us: on_device(): jnp.einsum('pl,skl->spk', current, blocks, precision=FULL_PRECISION)]
    psum x2 -> x0, waiting for transfers between devices: 40.3 us -> none  [on_device(): column_total = lax.psum(downward + mine, 'row')]
    another operation x20 -> x0, other arithmetic: 20.8 us -> none  [the longest x9 10.9 us: normalize(): factor = jnp.linalg.cholesky(mean_inner(block, block))]
  transfers between devices with their start and end apart: 6 -> 0, of which waited for: 6 -> 0; matrix products, arithmetic and copies ran while one was open for 5% -> 0% of each run, Pallas kernels for 0% -> 0%
where the time goes in v1:
time: 66 us; the launch traced here: 65.3 us
  Pallas kernels  61.8 us (94%)
  local copies, waits for them, and re-layouts  2.95 us (4%)
    pallas_call x1, Pallas kernels, on_device(): pl.pallas_call(functools.partial(kernel, rows, cols, group), out_shape=(j...  61.8 us
    unnamed x2, local copies, waits for them, and re-layouts  2.95 us

profile of v1, /device:TPU:0, one launch (start us, length us, event | category | flops | bytes accessed | tf_op | source)
XLA Modules:
  0.0 65.3 jit_solution(237033658362599874)
XLA Ops:
  0.6 61.8 %shard_map.50 = (f32[2,2,32,32]{3,2,1,0:T(8,128)}, f32[32,512]{1,0:T(8,128)}) custom-call(f32[32,512]{1,0:T(8,128)} %x_ref.1, f32[1,512]{1,0:T(1,128)} %bitcast.1, f32[8,1,512,512]{3,2,1,0:T(8,128)} %h_ref.1), custom_call_target="tpu_custom_call" | custom-call | tf_op jit(solution)/shard_map/pallas_call | solution.py:406
  62.4 1.5 %copy.7 = f32[2,2,32,32]{3,2,1,0:T(8,128)} copy(f32[2,2,32,32]{3,2,1,0:T(8,128)} %get-tuple-element.4) | data formatting | bytes 32768
  63.9 1.5 %copy.8 = f32[32,512]{1,0:T(8,128)} copy(f32[32,512]{1,0:T(8,128)} %get-tuple-element.5) | data formatting | bytes 131072

commit v2 on v1

--- a/solution.py
+++ b/solution.py
@@ -9,6 +9,8 @@
 
 ITERS = 2
 LANES = 128
+CORES = 2
+LAG = 2
 MESH = pl.DeviceIdType.MESH
 F32 = jnp.float32
 BF16 = jnp.bfloat16
@@ -59,8 +61,8 @@
 def kernel(
     rows, cols, group,
     x_ref, e_ref, h_ref, rec_ref, next_ref,
-    h_buf, h_high, h_low, lhs_buf, w_buf, gathered, across_out, across_in, acc, own, row_parts, gram_one, gram_two,
-    h_sem, gather_send, gather_recv, across_send, across_recv, row_send, row_recv, one_send, one_recv, two_send, two_recv,
+    h_buf, h_high, h_low, lhs_buf, w_buf, gathered, across_out, across_in, pair_in, acc, own, row_parts, gram_one, gram_two,
+    h_sem, gather_send, gather_recv, relay_send, pair_send, pair_recv, across_send, across_recv, row_send, row_recv, one_send, one_recv, two_send, two_recv,
 ):
     r, c = lax.axis_index("row"), lax.axis_index("col")
     slots = h_ref.shape[0]
@@ -68,6 +70,9 @@
     length = F32(cols * width)
     member, team = c % group, c // group
     teams = cols // group
+    chip, core = c // CORES, c % CORES
+    chips = cols // CORES
+    partner = chip * CORES + 1 - core
     is_owner = (c % rows) == r
     row = lax.broadcasted_iota(jnp.int32, (vecs, LANES), 0)
     lane = lax.broadcasted_iota(jnp.int32, (vecs, LANES), 1)
@@ -179,17 +184,42 @@
             gathered.at[app, i], gathered.at[app, i], gather_send.at[app, 0], gather_recv.at[app, i], (r, i * rows + r)
         )
 
+    def relay_copy(app, i):
+        return remote(
+            gathered.at[app, i], gathered.at[app, i], relay_send.at[app, i], gather_recv.at[app, i], (r, partner)
+        )
+
+    def pair_copy(app, i):
+        return remote(
+            across_out.at[app, i], pair_in.at[app, i], pair_send.at[app, i], pair_recv.at[app, i], (r, partner)
+        )
+
     def across_copy(app, i):
         return remote(
-            across_out.at[app, i], across_in.at[app, c], across_send.at[app, i], across_recv.at[app, c],
+            across_out.at[app, i], across_in.at[app, chip], across_send.at[app, i], across_recv.at[app, chip],
             (r, i * rows + r),
         )
 
     def across_wait(app, other):
         return remote(
             across_in.at[app, other], across_in.at[app, other], across_send.at[app, 0], across_recv.at[app, other],
-            (r, other),
-        )
+            (r, partner),
+        )
+
+    def leaves_chip(i):
+        return (i * rows + r) // CORES < chip
+
+    def is_relayed(i):
+        return leaves_chip(i) & ((i * rows + r) % CORES == core)
+
+    def goes_to_partner(i):
+        return leaves_chip(i) & (i % CORES != core)
+
+    def is_finished_here(i):
+        return leaves_chip(i) & (i % CORES == core)
+
+    def stays_on_chip(i):
+        return (i * rows + r < c) & ((i * rows + r) // CORES == chip)
 
     def row_copy(app, other):
         return remote(
@@ -201,18 +231,44 @@
             row_parts.at[app, other], row_parts.at[app, other], row_send.at[app, other], row_recv.at[app, other],
             (other, c),
         )
+
+    def targets(body):
+        @pl.when(is_owner)
+        def _():
+            @loop(chips - 1 - chip)
+            def _(step):
+                body((chips - 1 - step) * CORES + core)
+
+            @pl.when(core == 0)
+            def _():
+                body(partner)
 
     def send_block(app, src):
         @pl.when(is_owner)
         def _():
             gathered[app, c // rows] = 0.5 * src[...]
 
-            @loop(cols, c + 1)
-            def _(other):
-                gather_copy(app, src, other).start()
+        targets(lambda other: gather_copy(app, src, other).start())
+
+    def split_blocks():
+        @loop(slots)
+        def _(i):
+            @pl.when(i * rows + r <= c)
+            def _():
+                h_copy(i).wait()
+                high, low = split(h_buf[i])
+                h_high[i] = high
+                h_low[i] = low
 
     def send_across(app, src):
         lhs_buf[...] = stacked_split(src[...])
+
+        def finish(i):
+            @pl.when(is_finished_here(i))
+            def _():
+                pair_copy(app, i).wait_recv()
+                across_out[app, i] += pair_in[app, i]
+                across_copy(app, i).start()
 
         @loop(slots)
         def _(i):
@@ -220,34 +276,46 @@
 
             @pl.when(block_row <= c)
             def _():
-                if app == 0:
-                    h_copy(i).wait()
-                    high, low = split(h_buf[i])
-                    h_high[i] = high
-                    h_low[i] = low
-                else:
-                    high, low = h_high[i], h_low[i]
-                piece = three_products(lhs_buf[...], high, low, ((1,), (1,)))
+                piece = three_products(lhs_buf[...], h_high[i], h_low[i], ((1,), (1,)))
 
                 @pl.when(block_row < c)
                 def _():
                     across_out[app, i] = piece
+
+                @pl.when(goes_to_partner(i))
+                def _():
+                    pair_copy(app, i).start()
+
+                @pl.when(stays_on_chip(i))
+                def _():
                     across_copy(app, i).start()
 
                 @pl.when(block_row == c)
                 def _():
                     own[...] = 0.5 * piece
 
+            @pl.when(i >= LAG)
+            def _():
+                finish(i - LAG)
+
+        for step in range(min(LAG, slots)):
+            finish(slots - min(LAG, slots) + step)
+
     def downward(app):
         acc[...] = jnp.zeros_like(acc)
 
         @loop(slots)
-        def _(i):
+        def _(step):
+            i = slots - 1 - step
             block_row = i * rows + r
 
             @pl.when(block_row < c)
             def _():
                 gather_wait(app, i).wait_recv()
+
+            @pl.when(is_relayed(i))
+            def _():
+                relay_copy(app, i).start()
 
             @pl.when(block_row <= c)
             def _():
@@ -260,7 +328,7 @@
         def _():
             acc[...] += own[...]
 
-            @loop(cols, c + 1)
+            @loop(chips, chip + core)
             def _(other):
                 across_wait(app, other).wait_recv()
                 acc[...] += across_in[app, other]
@@ -319,6 +387,7 @@
     zero_block = jnp.zeros_like(start)
     local = gram_pair(start, zero_block) + jnp.where(lane == 2 * vecs, jnp.sum(energy) / length, 0.0)
 
+    split_blocks()
     pl.semaphore_wait(barrier, cols - 1 + rows - 1)
     send_block(0, x_ref)
     gram_start(0, local)
@@ -357,15 +426,19 @@
     for app in range(ITERS):
         source = x_ref if app == 0 else w_buf
 
-        @pl.when(is_owner)
-        def _():
-            @loop(cols, c + 1)
-            def _(other):
-                gather_copy(app, source, other).wait_send()
+        targets(lambda other: gather_copy(app, source, other).wait_send())
 
         @loop(slots)
         def _(i):
-            @pl.when(i * rows + r < c)
+            @pl.when(is_relayed(i))
+            def _():
+                relay_copy(app, i).wait_send()
+
+            @pl.when(goes_to_partner(i))
+            def _():
+                pair_copy(app, i).wait_send()
+
+            @pl.when(is_finished_here(i) | stays_on_chip(i))
             def _():
                 across_copy(app, i).wait_send()
 
@@ -419,7 +492,8 @@
                 pltpu.VMEM(block, F32),
                 pltpu.VMEM((ITERS, slots) + block, F32),
                 pltpu.VMEM((ITERS, slots) + block, F32),
-                pltpu.VMEM((ITERS, cols) + block, F32),
+                pltpu.VMEM((ITERS, cols // CORES) + block, F32),
+                pltpu.VMEM((ITERS, slots) + block, F32),
                 pltpu.VMEM(block, F32),
                 pltpu.VMEM(block, F32),
                 pltpu.VMEM((ITERS, rows) + block, F32),
@@ -429,7 +503,10 @@
                 dma((ITERS, cols)),
                 dma((ITERS, slots)),
                 dma((ITERS, slots)),
-                dma((ITERS, cols)),
+                dma((ITERS, slots)),
+                dma((ITERS, slots)),
+                dma((ITERS, slots)),
+                dma((ITERS, cols // CORES)),
                 dma((ITERS, rows)),
                 dma((ITERS, rows)),
                 dma((grams, group)),

time: 66 us -> 56.6 us (0.86)
  Pallas kernels: 61.8 us -> 52.7 us
    pallas_call x1, Pallas kernels: 61.8 us -> 52.7 us  [on_device(): pl.pallas_call(functools.partial(kernel, rows, cols, group), out_shape=(j...]
where the time goes in v2:
time: 56.6 us; the launch traced here: 56.3 us
  Pallas kernels  52.7 us (93%)
  local copies, waits for them, and re-layouts  2.95 us (5%)
  between operations  0.64 us (1%)
    pallas_call x1, Pallas kernels, on_device(): pl.pallas_call(functools.partial(kernel, rows, cols, group), out_shape=(j...  52.7 us
    unnamed x2, local copies, waits for them, and re-layouts  2.95 us

profile of v2, /device:TPU:0, one launch (start us, length us, event | category | flops | bytes accessed | tf_op | source)
XLA Modules:
  0.0 56.3 jit_solution(6554145947916699860)
XLA Ops:
  0.6 52.7 %shard_map.50 = (f32[2,2,32,32]{3,2,1,0:T(8,128)}, f32[32,512]{1,0:T(8,128)}) custom-call(f32[32,512]{1,0:T(8,128)} %x_ref.1, f32[1,512]{1,0:T(1,128)} %bitcast.1, f32[8,1,512,512]{3,2,1,0:T(8,128)} %h_ref.1), custom_call_target="tpu_custom_call" | custom-call | tf_op jit(solution)/shard_map/pallas_call | solution.py:479
  53.4 1.5 %copy.7 = f32[2,2,32,32]{3,2,1,0:T(8,128)} copy(f32[2,2,32,32]{3,2,1,0:T(8,128)} %get-tuple-element.4) | data formatting | bytes 32768
  54.8 1.5 %copy.8 = f32[32,512]{1,0:T(8,128)} copy(f32[32,512]{1,0:T(8,128)} %get-tuple-element.5) | data formatting | bytes 131072

commit v3 on v2

--- a/solution.py
+++ b/solution.py
@@ -48,14 +48,19 @@
 
 def factor_and_inverse(gram, row, lane, vecs):
     work = jnp.where(lane < vecs, gram, (lane - vecs == row).astype(F32))
-    for step in range(vecs):
-        scale = lax.rsqrt(work[step : step + 1, step : step + 1])
-        pivot_row = work[step : step + 1, :] * scale
-        column = work[:, step : step + 1] * scale
-        work = jnp.where(
-            row > step, work - column * pivot_row, jnp.where(row == step, pivot_row, work)
-        )
-    return work
+    for step in range(0, vecs, 2):
+        top, low = work[step : step + 1, :], work[step + 1 : step + 2, :]
+        left, right = work[:, step : step + 1], work[:, step + 1 : step + 2]
+        first, cross = top[:, step : step + 1], top[:, step + 1 : step + 2]
+        second = low[:, step + 1 : step + 2]
+        inverse = 1.0 / first
+        ratio = cross * inverse
+        low = low - ratio * top
+        right = right - ratio * left
+        reduced = work - left * (top * inverse) - right * (low * (1.0 / (second - cross * ratio)))
+        work = jnp.where(row > step + 1, reduced, jnp.where(row == step + 1, low, work))
+    pivots = jnp.sum(jnp.where(lane == row, work, 0.0), axis=1, keepdims=True)
+    return work * lax.rsqrt(pivots)
 
 
 def kernel(
@@ -394,11 +399,11 @@
     send_across(0, x_ref)
     gram_middle(0)
     downward(0)
+    collect(0)
     pair = gram_end(0)
     sigma = pair[0:1, 2 * vecs : 2 * vecs + 1]
     work = factor_and_inverse(pair, row, lane, vecs)
     current = apply_second(work, start)
-    collect(0)
     image = apply_second(work, row_total(0) + energy * start)
     w_buf[...] = image - sigma * current
 
@@ -408,11 +413,11 @@
     send_across(1, w_buf)
     gram_middle(1)
     downward(1)
+    collect(1)
     pair = gram_end(1)
     work = factor_and_inverse(residual_gram(pair), row, lane, vecs)
     record(0, pair, work, sigma)
     following = apply_second(work, shifted - apply_second(pair, current))
-    collect(1)
     w_image = row_total(1) + energy * shifted
     following_image = apply_second(work, w_image - apply_second(pair, image))
     last = following_image - apply_first(work, current) - sigma * following

time: 56.6 us -> 51.7 us (0.913)
  Pallas kernels: 52.7 us -> 47.8 us
    pallas_call x1, Pallas kernels: 52.7 us -> 47.8 us  [on_device(): pl.pallas_call(functools.partial(kernel, rows, cols, group), out_shape=(j...]
where the time goes in v3:
time: 51.7 us; the launch traced here: 51.4 us
  Pallas kernels  47.8 us (92%)
  local copies, waits for them, and re-layouts  2.95 us (6%)
  between operations  0.64 us (1%)
    pallas_call x1, Pallas kernels, on_device(): pl.pallas_call(functools.partial(kernel, rows, cols, group), out_shape=(j...  47.8 us
    unnamed x2, local copies, waits for them, and re-layouts  2.95 us

profile of v3, /device:TPU:0, one launch (start us, length us, event | category | flops | bytes accessed | tf_op | source)
XLA Modules:
  0.0 51.4 jit_solution(8522552791619546831)
XLA Ops:
  0.6 47.8 %shard_map.50 = (f32[2,2,32,32]{3,2,1,0:T(8,128)}, f32[32,512]{1,0:T(8,128)}) custom-call(f32[32,512]{1,0:T(8,128)} %x_ref.1, f32[1,512]{1,0:T(1,128)} %bitcast.1, f32[8,1,512,512]{3,2,1,0:T(8,128)} %h_ref.1), custom_call_target="tpu_custom_call" | custom-call | tf_op jit(solution)/shard_map/pallas_call | solution.py:484
  48.4 1.5 %copy.7 = f32[2,2,32,32]{3,2,1,0:T(8,128)} copy(f32[2,2,32,32]{3,2,1,0:T(8,128)} %get-tuple-element.4) | data formatting | bytes 32768
  49.9 1.5 %copy.8 = f32[32,512]{1,0:T(8,128)} copy(f32[32,512]{1,0:T(8,128)} %get-tuple-element.5) | data formatting | bytes 131072

commit v4 on v3

--- a/solution.py
+++ b/solution.py
@@ -416,12 +416,12 @@
     collect(1)
     pair = gram_end(1)
     work = factor_and_inverse(residual_gram(pair), row, lane, vecs)
+    following = apply_second(work, shifted - apply_second(pair, current))
+    known_image = energy * shifted - apply_second(pair, image)
+    known_last = apply_first(work, current) + sigma * following
+    last = apply_second(work, row_total(1) + known_image) - known_last
+    gram_start(2, gram_pair(last, following))
     record(0, pair, work, sigma)
-    following = apply_second(work, shifted - apply_second(pair, current))
-    w_image = row_total(1) + energy * shifted
-    following_image = apply_second(work, w_image - apply_second(pair, image))
-    last = following_image - apply_first(work, current) - sigma * following
-    gram_start(2, gram_pair(last, following))
     gram_middle(2)
     pair = gram_end(2)
     work = factor_and_inverse(residual_gram(pair), row, lane, vecs)

time: 51.7 us -> 51.6 us (level)
  no operation moved by 1% of the time
where the time goes in v4:
time: 51.6 us; the launch traced here: 51.3 us
  Pallas kernels  47.7 us (92%)
  local copies, waits for them, and re-layouts  2.95 us (6%)
  between operations  0.64 us (1%)
    pallas_call x1, Pallas kernels, on_device(): pl.pallas_call(functools.partial(kernel, rows, cols, group), out_shape=(j...  47.7 us
    unnamed x2, local copies, waits for them, and re-layouts  2.95 us

profile of v4, /device:TPU:0, one launch (start us, length us, event | category | flops | bytes accessed | tf_op | source)
XLA Modules:
  0.0 51.3 jit_solution(14121824510984573218)
XLA Ops:
  0.6 47.7 %shard_map.50 = (f32[2,2,32,32]{3,2,1,0:T(8,128)}, f32[32,512]{1,0:T(8,128)}) custom-call(f32[32,512]{1,0:T(8,128)} %x_ref.1, f32[1,512]{1,0:T(1,128)} %bitcast.1, f32[8,1,512,512]{3,2,1,0:T(8,128)} %h_ref.1), custom_call_target="tpu_custom_call" | custom-call | tf_op jit(solution)/shard_map/pallas_call | solution.py:484
  48.3 1.5 %copy.7 = f32[2,2,32,32]{3,2,1,0:T(8,128)} copy(f32[2,2,32,32]{3,2,1,0:T(8,128)} %get-tuple-element.4) | data formatting | bytes 32768
  49.8 1.5 %copy.8 = f32[32,512]{1,0:T(8,128)} copy(f32[32,512]{1,0:T(8,128)} %get-tuple-element.5) | data formatting | bytes 131072
